TPU v7x, 256 devices: a whole 4x4x8 slice. The times are simulated.
256 devices in a mesh: pipe: 2 (over core), dp: 128 (over x, y, z).
Axes of the slice: x: 4, y: 4, z: 8, core: 2. Of those that a mesh axis runs over, the one named last changes fastest.
Arguments:
- tokens: bfloat16 [4, 4096, 2048], P(None, 'dp'), may hold values from -40 to 40
- seg_ids: int32 [4, 4096], P(None, 'dp'), may hold values from 0 to 31, as said below
- cache_row: int32 [4, 4096], P(None, 'dp'), may hold values from 0 to 16383, as said below
- ln_gain: float32 [2, 2048], P('pipe'), may hold values from 0.1 to 1.9
- ln_bias: float32 [2, 2048], P('pipe'), may hold values from -2 to 2
- qkv_weight: bfloat16 [2, 2048, 3072], P('pipe', 'dp'), may hold values from -8 to 8
- qkv_bias: float32 [2, 3072], P('pipe'), may hold values from -3 to 3
- out_weight: bfloat16 [2, 1024, 2048], P('pipe', 'dp'), may hold values from -0.1875 to 0.1875
- out_bias: float32 [2, 2048], P('pipe'), may hold values from -2 to 2
Outputs:
- hidden: bfloat16 [2, 4, 4096, 2048], P('pipe', None, 'dp')
- kv_cache: bfloat16 [2, 16384, 2048], P('pipe', 'dp')
Inputs may be any that keep to these rules, and one draw needn't show every extreme that they name: `seg_ids`: each block of 32 tokens of a micro-batch holds whole prompts, numbered from 0 in order, never crossing the block's edges. In every micro-batch one block holds a single prompt of 32 tokens and another holds 32 prompts of one token. `cache_row`: over all micro-batches each cache row is named once. Rows d * 4 * 32 to (d + 1) * 4 * 32 - 1 belong to index d of dp, which gets 32 of them in each micro-batch. Of the 32 tokens of one index of dp in one micro-batch, each owner gets none or exactly 2.
All inputs are finite; a program needn't handle non-finite values.
Results may differ from a plain program's by a relative error of at most 0.0065.
Values may be sent and summed in bfloat16 or wider, within the bound.
No kernel may reach another device: no remote copies, remote signals or barrier semaphores. Data moves between devices by JAX's collectives and lax.ppermute only.
A program may use at most 128 MiB of HBM per device.

v0:
```python
import jax
import jax.numpy as jnp
from jax import lax
from jax.sharding import PartitionSpec as P

HEADS = 4
HDIM = 256
ROT = 64
HALF = ROT // 2
EPS = 1e-05
META = 128
BF = jnp.bfloat16
F32 = jnp.float32


def swap(value):
    return lax.ppermute(value, "pipe", [(0, 1), (1, 0)])


def mm(a, b):
    return jnp.dot(a, b, preferred_element_type=F32)


def layer_norm(layer_in, gain_row, shift_row):
    data = layer_in.astype(F32)
    centre = jnp.mean(data, axis=-1, keepdims=True)
    centred = data - centre
    variance = jnp.mean(centred * centred, axis=-1, keepdims=True)
    return (centred * lax.rsqrt(variance + EPS) * gain_row + shift_row).astype(BF)


def angles_of(positions):
    inverse = 10000.0 ** (-2.0 * jnp.arange(HALF, dtype=F32) / ROT)
    angles = positions[:, None] * inverse[None, :]
    return (jnp.cos(angles), jnp.sin(angles))


def rotary(head_cols, cos_sin):
    cosine, sine = cos_sin
    out = []
    for first in range(0, head_cols.shape[1], HDIM):
        leading = head_cols[:, first : first + HALF]
        trailing = head_cols[:, first + HALF : first + ROT]
        out += [
            leading * cosine - trailing * sine,
            trailing * cosine + leading * sine,
            head_cols[:, first + ROT : first + HDIM],
        ]
    return jnp.concatenate(out, axis=-1)


def attend(queries, key_rows, value_rows, allowed):
    parts = []
    for first in range(0, queries.shape[1], HDIM):
        one = slice(first, first + HDIM)
        scores = lax.dot_general(
            queries[:, one], key_rows[:, one], (((1,), (1,)), ((), ())), preferred_element_type=F32
        ) * HDIM ** (-0.5)
        scores = jnp.where(allowed, scores, -1e30)
        exp_scores = jnp.exp(scores - jnp.max(scores, axis=-1, keepdims=True))
        probs = (exp_scores / jnp.sum(exp_scores, axis=-1, keepdims=True)).astype(BF)
        parts.append(mm(probs, value_rows[:, one]).astype(BF))
    return jnp.concatenate(parts, axis=-1)


def shards(
    tokens, seg_ids, cache_row, ln_gain, ln_bias, qkv_weight, qkv_bias, out_weight, out_bias
):
    micro_count, row_count, width = tokens.shape
    device_count = lax.axis_size("dp")
    core = lax.axis_index("pipe")
    first_core = core == 0
    cache_size = micro_count * row_count
    slot_cap = 2 * micro_count * ((row_count + device_count - 1) // device_count)
    head_width = qkv_weight.shape[2] // 3
    half_heads = head_width // 2
    half_width = width // 2

    def pick(a, b):
        return jnp.where(first_core, a, b)

    qkv_shard = qkv_weight[0].reshape(-1, 3, 2, half_heads)
    out_shard = out_weight[0]

    def packed(which):
        qkv_part = qkv_shard[:, :, which, :].reshape(-1, 3 * half_heads)
        out_part = out_shard[:, which * half_width : (which + 1) * half_width]
        out_part = jnp.concatenate(
            [out_part[:, : half_width // 2], out_part[:, half_width // 2 :]], axis=0
        )
        return jnp.concatenate([qkv_part, out_part], axis=1)

    low, high = (packed(0), packed(1))
    kept = pick(low, high)
    got = swap(pick(high, low))
    both = jnp.concatenate([pick(kept, got), pick(got, kept)], axis=1)
    gathered = lax.all_gather(both, "dp", axis=0, tiled=True)
    vectors = jnp.concatenate([ln_gain[0], ln_bias[0], qkv_bias[0], out_bias[0]])
    vectors_got = swap(vectors)
    vectors_of = (pick(vectors, vectors_got), pick(vectors_got, vectors))

    def weights_of(layer):
        begin = layer * 2 * head_width
        qkv = gathered[:, begin : begin + 3 * half_heads]
        out = gathered[:, begin + 3 * half_heads : begin + 2 * head_width]
        out = out.reshape(device_count, 2, -1, half_heads)
        out = jnp.concatenate(
            [out[:, 0].reshape(head_width, half_heads), out[:, 1].reshape(head_width, half_heads)],
            axis=1,
        )
        other = swap(out)
        out = jnp.concatenate([pick(out, other), pick(other, out)], axis=1)
        vec = vectors_of[layer]
        gain = vec[:width]
        shift = vec[width : 2 * width]
        bias = vec[2 * width : 2 * width + 3 * head_width].reshape(3, 2, half_heads)
        bias = pick(bias[:, 0], bias[:, 1]).reshape(-1)
        out_b = vec[2 * width + 3 * head_width :]
        return (qkv, bias, out, out_b, gain, shift)

    flat = tokens.reshape(cache_size, width)
    seg = seg_ids.reshape(cache_size)
    rows = cache_row.reshape(cache_size)
    order = jnp.arange(cache_size, dtype=jnp.int32)
    micro = order // row_count
    same_micro = micro[:, None] == micro[None, :]
    positions = order % row_count - jnp.sum(
        (same_micro & (seg[None, :] < seg[:, None])).astype(jnp.int32), axis=1
    )
    earlier = order[None, :] <= order[:, None]
    allowed = same_micro & earlier & (seg[:, None] == seg[None, :])
    owners = rows // cache_size
    rank = (
        jnp.sum(
            (same_micro & earlier & (owners[:, None] == owners[None, :])).astype(jnp.int32), axis=1
        )
        - 1
    )
    slot = owners * slot_cap + micro * (slot_cap // micro_count) + rank
    slots = device_count * slot_cap
    send = (jnp.arange(slots, dtype=jnp.int32)[:, None] == slot[None, :]).astype(BF)

    def exchange(payload):
        cols = payload.shape[1]
        filled = mm(send, payload).astype(BF).reshape(device_count, slot_cap, cols)
        arrived = lax.all_to_all(filled, "dp", split_axis=0, concat_axis=0, tiled=True)
        return arrived.reshape(slots, cols)

    lane = jnp.arange(META, dtype=jnp.int32)[None, :]
    meta = jnp.where(
        lane == 0, (rows % cache_size + 1)[:, None], jnp.where(lane == 1, positions[:, None], 0)
    ).astype(BF)
    half_tokens = pick(flat[:, :half_width], flat[:, half_width:])
    arrived = exchange(jnp.concatenate([half_tokens, meta], axis=1))
    place = arrived[:, half_width].astype(jnp.int32) - 1
    take = (order[:, None] == place[None, :]).astype(BF)
    own = mm(take, arrived).astype(BF)
    own_half = own[:, :half_width]
    own_other = swap(own_half)
    own_tokens = jnp.concatenate([pick(own_half, own_other), pick(own_other, own_half)], axis=1)
    turn = angles_of(positions.astype(F32))
    own_turn = angles_of(own[:, half_width + 1].astype(F32))

    def keys_values(layer_in, weights, cos_sin):
        qkv, bias, _, _, gain, shift = weights
        normed = layer_norm(layer_in, gain, shift)
        projected = mm(normed, qkv[:, half_heads:]) + bias[half_heads:]
        return jnp.concatenate(
            [rotary(projected[:, :half_heads], cos_sin), projected[:, half_heads:]], axis=1
        ).astype(BF)

    def context_of(layer_in, weights):
        qkv, bias, _, _, gain, shift = weights
        normed = layer_norm(layer_in, gain, shift)
        projected = mm(normed, qkv) + bias
        queries = rotary(projected[:, :half_heads], turn).astype(BF)
        key_rows = rotary(projected[:, half_heads : 2 * half_heads], turn).astype(BF)
        return attend(queries, key_rows, projected[:, 2 * half_heads :].astype(BF), allowed)

    def finish(layer_in, context_half, weights):
        other = swap(context_half)
        context = jnp.concatenate([pick(context_half, other), pick(other, context_half)], axis=1)
        return (layer_in.astype(F32) + mm(context, weights[2]) + weights[3]).astype(BF)

    layer0, layer1 = (weights_of(0), weights_of(1))
    context0 = context_of(flat, layer0)
    own_context0 = mm(take, exchange(context0)).astype(BF)
    hidden0 = finish(flat, context0, layer0)
    own_kv0 = keys_values(own_tokens, layer0, own_turn)
    context1 = context_of(hidden0, layer1)
    hidden1 = finish(hidden0, context1, layer1)
    own_hidden0 = finish(own_tokens, own_context0, layer0)
    own_kv1 = keys_values(own_hidden0, layer1, own_turn)
    kept_kv = pick(own_kv0, own_kv1)
    got_kv = swap(pick(own_kv1, own_kv0))
    low_kv, high_kv = (pick(kept_kv, got_kv), pick(got_kv, kept_kv))
    cache = jnp.concatenate(
        [
            low_kv[:, :half_heads],
            high_kv[:, :half_heads],
            low_kv[:, half_heads:],
            high_kv[:, half_heads:],
        ],
        axis=1,
    )
    hidden = pick(hidden0, hidden1).reshape(1, micro_count, row_count, width)
    return (hidden, cache[None])


def solution(mesh):
    placed = (
        P(None, "dp", None),
        P(None, "dp"),
        P(None, "dp"),
        P("pipe", None),
        P("pipe", None),
        P("pipe", "dp", None),
        P("pipe", None),
        P("pipe", "dp", None),
        P("pipe", None),
    )
    return jax.shard_map(
        shards,
        mesh=mesh,
        in_specs=placed,
        out_specs=(P("pipe", None, "dp", None), P("pipe", "dp", None)),
        check_vma=False,
    )
```

profile of v0, /device:TPU:1, one launch (start us, length us, event | category | flops | bytes accessed | tf_op | source)
XLA Modules:
  0.0 268.0 jit_solution(13999180450505885761)
XLA Ops:
  8.0 0.9 reshape_squeeze.21
  9.5 3.3 %collective-permute-start.1 = (bf16[16,2048]{1,0:T(8,128)(2,1)S(1)}, bf16[16,2048]{1,0:T(8,128)(2,1)S(1)}, u32[]{:S(2)}, u32[]{:S(2)}) collective-permute-start(bf16[16,2048]{1,0:T(8,128)(2,1)S(1)} %broadcast_select_fusion.18), channel_id=1, source_target_pairs={{0,128},{128,0},{1,129},{129,1},{2,130},{130,2},{3,131},{131,3},{4... | collective-permute-start | bytes 196616 | tf_op jit(solution)/shard_map/ppermute | solution.py:17
  12.8 0.9 collective-permute-done.1
  14.4 1.3 copy.29
  15.8 1.0 reshape.338
  17.9 2.2 fusion.12
  20.1 13.8 %all-to-all-start = ((bf16[128,8,1152]{2,1,0:T(8,128)(2,1)}), bf16[128,8,1152]{2,1,0:T(8,128)(2,1)S(1)}, u32[]{:S(2)}, u32[]{:S(2)}) async-start(bf16[128,8,1152]{2,1,0:T(8,128)(2,1)} %fusion.12), calls=%async_computation | async-start | bytes 4718592 | tf_op jit(solution)/shard_map/all_to_all | solution.py:146
  36.2 66.5 %all-to-all-done = bf16[128,8,1152]{2,1,0:T(8,128)(2,1)S(1)} async-done(((bf16[128,8,1152]{2,1,0:T(8,128)(2,1)}), bf16[128,8,1152]{2,1,0:T(8,128)(2,1)S(1)}, u32[]{:S(2)}, u32[]{:S(2)}) %all-to-all-start) | async-done | bytes 2359328 | tf_op jit(solution)/shard_map/all_to_all | solution.py:146
  103.0 1.0 convolution_convert_fusion.1
  104.0 3.3 %collective-permute-start.6 = (bf16[128,1024]{0,1:T(8,128)(2,1)S(1)}, bf16[128,1024]{0,1:T(8,128)(2,1)S(1)}, u32[]{:S(2)}, u32[]{:S(2)}) collective-permute-start(bf16[128,1024]{0,1:T(8,128)(2,1)S(1)} %slice.489), channel_id=1, source_target_pairs={{0,128},{128,0},{1,129},{129,1},{2,130},{130,2},{3,131},{131,3},{4... | collective-permute-start | bytes 786440 | tf_op jit(solution)/shard_map/ppermute | solution.py:17
  109.7 69.0 %all-gather.2.cloned.1.call-done = bf16[2048,4096]{1,0:T(8,128)(2,1)} async-done(((bf16[16,4096]{1,0:T(8,128)(2,1)}), bf16[2048,4096]{1,0:T(8,128)(2,1)}) %all-gather.2.cloned.1.call-update) | async-done | bytes 16777232 | tf_op jit(solution)/shard_map/all_gather | solution.py:97
  178.7 5.6 %fusion.281 = (bf16[128,1536]{0,1:T(8,128)(2,1)S(1)}, f32[128,1536]{0,1:T(8,128)S(1)}) fusion(f32[1536]{0:T(1024)S(1)} %select_n.239, bf16[2048,4096]{1,0:T(8,128)(2,1)} %all-gather.2.cloned.1.call-done, bf16[128,2048]{0,1:T(8,128)(2,1)} %copy-done.5, f32[2048]{0:T(1024)S(1)} %get-tuple-element.73, f32[2048]{0:T(1024)S(1)} %get-tuple-element.71, ...), kind=kOutput, calls=%fused_computation.381 | convolution fusion | flops 807272448 | bytes 8018944 | tf_op jit(solution)/shard_map/dot_general | solution.py:21
  185.5 1.4 fusion.40
  186.9 10.2 %all-to-all-start.1 = ((bf16[128,8,512]{2,1,0:T(8,128)(2,1)}), bf16[128,8,512]{2,1,0:T(8,128)(2,1)}, u32[]{:S(2)}, u32[]{:S(2)}) async-start(bf16[128,8,512]{2,1,0:T(8,128)(2,1)} %fusion.40), calls=%async_computation.1 | async-start | bytes 2097152 | tf_op jit(solution)/shard_map/all_to_all | solution.py:146
  197.1 2.5 fusion.273
  199.8 1.7 pad_maximum_fusion.17
  201.5 1.4 collective-permute-start.3
  203.7 1.7 pad_maximum_fusion.18
  205.9 5.1 %fusion.288 = (bf16[128,1024]{0,1:T(8,128)(2,1)}, f32[128,1024]{0,1:T(8,128)}) fusion(f32[1024]{0:T(1024)S(1)} %bitcast.61, bf16[2048,4096]{1,0:T(8,128)(2,1)} %all-gather.2.cloned.1.call-done, f32[128]{0:T(128)S(1)} %add_rsqrt_fusion.2, f32[128]{0:T(128)S(1)} %broadcast_multiply_fusion.2, f32[2048]{0:T(1024)S(1)} %copy-done.21, f32[2048]{0:T(1024)S(1)} %copy-done.19, ...), kind=kOutput, calls=%fused_computation.388 | convolution fusion | flops 539492352 | bytes 5526528 | tf_op jit(solution)/shard_map/dot_general | solution.py:21
  211.7 14.6 %all-to-all-done.1 = bf16[128,8,512]{2,1,0:T(8,128)(2,1)} async-done(((bf16[128,8,512]{2,1,0:T(8,128)(2,1)}), bf16[128,8,512]{2,1,0:T(8,128)(2,1)}, u32[]{:S(2)}, u32[]{:S(2)}) %all-to-all-start.1) | async-done | bytes 1048608 | tf_op jit(solution)/shard_map/all_to_all | solution.py:146
  226.3 1.5 convolution_convert_fusion.3
  227.9 3.6 %collective-permute-start.7 = (bf16[128,512]{1,0:T(8,128)(2,1)S(1)}, bf16[128,512]{1,0:T(8,128)(2,1)S(1)}, u32[]{:S(2)}, u32[]{:S(2)}) collective-permute-start(bf16[128,512]{1,0:T(8,128)(2,1)S(1)} %convolution_convert_fusion.3), channel_id=1, source_target_pairs={{0,128},{128,0},{1,129},{129,1},{2,130},{130,2},{3,131},{131,3},{4... | collective-permute-start | bytes 393224 | tf_op jit(solution)/shard_map/ppermute | solution.py:17
  231.5 3.0 %broadcast_select_fusion.3 = (bf16[1024,1024]{1,0:T(8,128)(2,1)S(1)}, bf16[1024,1024]{1,0:T(8,128)(2,1)S(1)}) fusion(bf16[1024,1024]{1,0:T(8,128)(2,1)} %collective-permute-done.3, pred[]{:T(512)S(6)} %eq.103, bf16[1024,512]{1,0:T(8,128)(2,1)} %copy-done, bf16[1024,512]{1,0:T(8,128)(2,1)S(1)} %get-tuple-element.24), kind=kLoop, calls=%fused_computation.36 | loop fusion | flops 6291456 | bytes 8388609 | tf_op jit(solution)/shard_map/jit(_where)/select_n | solution.py:80
  234.5 1.8 convert_reduce_fusion.1
  236.6 5.6 %fusion.284 = (bf16[128,1536]{0,1:T(8,128)(2,1)S(1)}, f32[128,1536]{0,1:T(8,128)S(1)}) fusion(f32[1536]{0:T(1024)S(1)} %select_n.250, bf16[2048,4096]{1,0:T(8,128)(2,1)} %all-gather.2.cloned.1.call-done, bf16[128,2048]{0,1:T(8,128)(2,1)S(1)} %get-tuple-element.95, f32[2048]{0:T(1024)S(1)} %copy-done.17, f32[2048]{0:T(1024)S(1)} %copy-done.16, ...), kind=kOutput, calls=%fused_computation.384 | convolution fusion | flops 807272448 | bytes 8018944 | tf_op jit(solution)/shard_map/dot_general | solution.py:21
  243.8 2.6 broadcast_select_fusion.1
  246.5 1.8 fusion.287
  248.6 4.2 %fusion.289 = (bf16[128,1024]{0,1:T(8,128)(2,1)S(1)}, f32[128,1024]{0,1:T(8,128)S(1)}) fusion(f32[1024]{0:T(1024)S(1)} %bitcast.60, bf16[2048,4096]{1,0:T(8,128)(2,1)} %all-gather.2.cloned.1.call-done, f32[128,2048]{0,1:T(8,128)S(1)} %get-tuple-element.103, f32[128]{0:T(128)S(1)} %add_rsqrt_fusion.1, f32[128]{0:T(128)S(1)} %broadcast_multiply_fusion.1, ...), kind=kOutput, calls=%fused_computation.389 | convolution fusion | flops 538443776 | bytes 6050816 | tf_op jit(solution)/shard_map/dot_general | solution.py:21
  253.7 0.9 constant_dynamic-update-slice_fusion.2
  257.2 1.8 fusion.37
  258.9 1.0 copy.36
  260.1 1.0 copy.43
  (161 shorter events, 17.2 us)
Async XLA Ops:
  7.2 171.5 %all-gather.2.cloned.1.call-start = ((), (), s32[]{:S(2)}) async-start(), calls=%async_computation.2 | async-start | bytes 16908288 | tf_op jit(solution)/shard_map/all_gather | solution.py:97
  9.5 4.2 %collective-permute-start.1 = (bf16[16,2048]{1,0:T(8,128)(2,1)S(1)}, bf16[16,2048]{1,0:T(8,128)(2,1)S(1)}, u32[]{:S(2)}, u32[]{:S(2)}) collective-permute-start(bf16[16,2048]{1,0:T(8,128)(2,1)S(1)} %broadcast_select_fusion.18), channel_id=1, source_target_pairs={{0,128},{128,0},{1,129},{129,1},{2,130},{130,2},{3,131},{131,3},{4... | collective-permute-start | bytes 196616 | tf_op jit(solution)/shard_map/ppermute | solution.py:17
  15.7 18.1 %copy-start.10 = (f32[1,3072]{1,0:T(1,128)S(1)}, f32[1,3072]{1,0:T(1,128)}, u32[]{:S(2)}) copy-start(f32[1,3072]{1,0:T(1,128)} %param.15) | copy-start | bytes 36868
  15.8 18.1 %copy-start.11 = (f32[1,2048]{1,0:T(1,128)S(1)}, f32[1,2048]{1,0:T(1,128)}, u32[]{:S(2)}) copy-start(f32[1,2048]{1,0:T(1,128)} %param.17) | copy-start | bytes 24580
  15.8 18.1 %copy-start.12 = (f32[1,2048]{1,0:T(1,128)S(1)}, f32[1,2048]{1,0:T(1,128)}, u32[]{:S(2)}) copy-start(f32[1,2048]{1,0:T(1,128)} %param.13) | copy-start | bytes 24580
  15.8 18.1 %copy-start.13 = (f32[1,2048]{1,0:T(1,128)S(1)}, f32[1,2048]{1,0:T(1,128)}, u32[]{:S(2)}) copy-start(f32[1,2048]{1,0:T(1,128)} %param.12) | copy-start | bytes 24580
  15.8 18.9 %copy-start.1 = (bf16[4,32,2048]{2,1,0:T(8,128)(2,1)S(1)}, bf16[4,32,2048]{2,1,0:T(8,128)(2,1)}, u32[]{:S(2)}) copy-start(bf16[4,32,2048]{2,1,0:T(8,128)(2,1)} %param.9) | copy-start | bytes 1572868
  17.5 167.5 %copy-start.23 = (s32[128]{0:T(128)}, s32[128]{0:T(128)S(1)}, u32[]{:S(2)}) copy-start(s32[128]{0:T(128)S(1)} %eq.107) | copy-start | bytes 1540
  17.6 167.5 %copy-start.25 = (s32[128]{0:T(128)}, s32[128]{0:T(128)S(1)}, u32[]{:S(2)}) copy-start(s32[128]{0:T(128)S(1)} %get-tuple-element.110) | copy-start | bytes 1540
  17.7 166.6 %copy-start.29 = (f32[128]{0:T(128)}, f32[128]{0:T(128)S(1)}, u32[]{:S(2)}) copy-start(f32[128]{0:T(128)S(1)} %get-tuple-element.12) | copy-start | bytes 1540
  20.1 82.6 %all-to-all-start = ((bf16[128,8,1152]{2,1,0:T(8,128)(2,1)}), bf16[128,8,1152]{2,1,0:T(8,128)(2,1)S(1)}, u32[]{:S(2)}, u32[]{:S(2)}) async-start(bf16[128,8,1152]{2,1,0:T(8,128)(2,1)} %fusion.12), calls=%async_computation | async-start | bytes 4718592 | tf_op jit(solution)/shard_map/all_to_all | solution.py:146
  33.9 1.6 collective-permute-start
  36.2 148.1 %copy-start.18 = (f32[2048]{0:T(1024)}, f32[2048]{0:T(1024)S(1)}, u32[]{:S(2)}) copy-start(f32[2048]{0:T(1024)S(1)} %get-tuple-element.71) | copy-start | bytes 24580
  36.2 148.1 %copy-start.20 = (f32[2048]{0:T(1024)}, f32[2048]{0:T(1024)S(1)}, u32[]{:S(2)}) copy-start(f32[2048]{0:T(1024)S(1)} %get-tuple-element.73) | copy-start | bytes 24580
  104.0 5.6 %collective-permute-start.6 = (bf16[128,1024]{0,1:T(8,128)(2,1)S(1)}, bf16[128,1024]{0,1:T(8,128)(2,1)S(1)}, u32[]{:S(2)}, u32[]{:S(2)}) collective-permute-start(bf16[128,1024]{0,1:T(8,128)(2,1)S(1)} %slice.489), channel_id=1, source_target_pairs={{0,128},{128,0},{1,129},{129,1},{2,130},{130,2},{3,131},{131,3},{4... | collective-permute-start | bytes 786440 | tf_op jit(solution)/shard_map/ppermute | solution.py:17
  109.7 93.4 %copy-start.2 = (bf16[128,1024]{0,1:T(8,128)(2,1)}, bf16[128,1024]{0,1:T(8,128)(2,1)S(1)}, u32[]{:S(2)}) copy-start(bf16[128,1024]{0,1:T(8,128)(2,1)S(1)} %get-tuple-element.45) | copy-start | bytes 786436
  186.9 39.3 %all-to-all-start.1 = ((bf16[128,8,512]{2,1,0:T(8,128)(2,1)}), bf16[128,8,512]{2,1,0:T(8,128)(2,1)}, u32[]{:S(2)}, u32[]{:S(2)}) async-start(bf16[128,8,512]{2,1,0:T(8,128)(2,1)} %fusion.40), calls=%async_computation.1 | async-start | bytes 2097152 | tf_op jit(solution)/shard_map/all_to_all | solution.py:146
  201.5 30.0 %collective-permute-start.3 = (bf16[1024,1024]{1,0:T(8,128)(2,1)}, bf16[1024,1024]{1,0:T(8,128)(2,1)}, u32[]{:S(2)}, u32[]{:S(2)}) collective-permute-start(bf16[1024,1024]{1,0:T(8,128)(2,1)} %pad_maximum_fusion.17), channel_id=1, source_target_pairs={{0,128},{128,0},{1,129},{129,1},{2,130},{130,2},{3,131},{131,3},{4... | collective-permute-start | bytes 6291464 | tf_op jit(solution)/shard_map/ppermute | solution.py:17
  203.4 7.5 %collective-permute-start.2 = (bf16[128,512]{1,0:T(8,128)(2,1)S(1)}, bf16[128,512]{1,0:T(8,128)(2,1)S(1)}, u32[]{:S(2)}, u32[]{:S(2)}) collective-permute-start(bf16[128,512]{1,0:T(8,128)(2,1)S(1)} %pad_maximum_fusion.21), channel_id=1, source_target_pairs={{0,128},{128,0},{1,129},{129,1},{2,130},{130,2},{3,131},{131,3},{4... | collective-permute-start | bytes 393224 | tf_op jit(solution)/shard_map/ppermute | solution.py:17
  205.4 38.4 %collective-permute-start.5 = (bf16[1024,1024]{1,0:T(8,128)(2,1)}, bf16[1024,1024]{1,0:T(8,128)(2,1)}, u32[]{:S(2)}, u32[]{:S(2)}) collective-permute-start(bf16[1024,1024]{1,0:T(8,128)(2,1)} %pad_maximum_fusion.18), channel_id=1, source_target_pairs={{0,128},{128,0},{1,129},{129,1},{2,130},{130,2},{3,131},{131,3},{4... | collective-permute-start | bytes 6291464 | tf_op jit(solution)/shard_map/ppermute | solution.py:17
  227.8 6.6 %copy-start.6 = (bf16[128,2048]{0,1:T(8,128)(2,1)S(1)}, bf16[128,2048]{0,1:T(8,128)(2,1)}, u32[]{:S(2)}) copy-start(bf16[128,2048]{0,1:T(8,128)(2,1)} %copy-done.5) | copy-start | bytes 1572868
  227.8 6.6 %copy-start.8 = (bf16[128,512]{1,0:T(8,128)(2,1)S(1)}, bf16[128,512]{1,0:T(8,128)(2,1)}, u32[]{:S(2)}) copy-start(bf16[128,512]{1,0:T(8,128)(2,1)} %get-tuple-element.62) | copy-start | bytes 393220
  227.8 6.6 %copy-start.9 = (bf16[128,512]{1,0:T(8,128)(2,1)S(1)}, bf16[128,512]{1,0:T(8,128)(2,1)}, u32[]{:S(2)}) copy-start(bf16[128,512]{1,0:T(8,128)(2,1)} %get-tuple-element.63) | copy-start | bytes 393220
  227.8 6.6 %copy-start.15 = (f32[2048]{0:T(1024)S(1)}, f32[2048]{0:T(1024)}, u32[]{:S(2)}) copy-start(f32[2048]{0:T(1024)} %get-tuple-element.72) | copy-start | bytes 24580
  227.9 18.6 %collective-permute-start.7 = (bf16[128,512]{1,0:T(8,128)(2,1)S(1)}, bf16[128,512]{1,0:T(8,128)(2,1)S(1)}, u32[]{:S(2)}, u32[]{:S(2)}) collective-permute-start(bf16[128,512]{1,0:T(8,128)(2,1)S(1)} %convolution_convert_fusion.3), channel_id=1, source_target_pairs={{0,128},{128,0},{1,129},{129,1},{2,130},{130,2},{3,131},{131,3},{4... | collective-permute-start | bytes 393224 | tf_op jit(solution)/shard_map/ppermute | solution.py:17
  236.6 5.6 %copy-start.30 = (f32[128]{0:T(128)S(1)}, f32[128]{0:T(128)}, u32[]{:S(2)}) copy-start(f32[128]{0:T(128)} %copy-done.29) | copy-start | bytes 1540
  236.6 5.8 %copy-start.24 = (s32[128]{0:T(128)S(1)}, s32[128]{0:T(128)}, u32[]{:S(2)}) copy-start(s32[128]{0:T(128)} %copy-done.23) | copy-start | bytes 1540
  236.6 5.8 %copy-start.26 = (s32[128]{0:T(128)S(1)}, s32[128]{0:T(128)}, u32[]{:S(2)}) copy-start(s32[128]{0:T(128)} %copy-done.25) | copy-start | bytes 1540
  243.4 13.7 %collective-permute-start.4 = (bf16[128,512]{1,0:T(8,128)(2,1)S(1)}, bf16[128,512]{1,0:T(8,128)(2,1)S(1)}, u32[]{:S(2)}, u32[]{:S(2)}) collective-permute-start(bf16[128,512]{1,0:T(8,128)(2,1)S(1)} %pad_maximum_fusion.22), channel_id=1, source_target_pairs={{0,128},{128,0},{1,129},{129,1},{2,130},{130,2},{3,131},{131,3},{4... | collective-permute-start | bytes 393224 | tf_op jit(solution)/shard_map/ppermute | solution.py:17
  248.3 6.3 %copy-start.7 = (bf16[128,1024]{0,1:T(8,128)(2,1)S(1)}, bf16[128,1024]{0,1:T(8,128)(2,1)}, u32[]{:S(2)}) copy-start(bf16[128,1024]{0,1:T(8,128)(2,1)} %get-tuple-element.104) | copy-start | bytes 786436
  248.6 8.6 %copy-start.14 = (f32[2048]{0:T(1024)S(1)}, f32[2048]{0:T(1024)}, u32[]{:S(2)}) copy-start(f32[2048]{0:T(1024)} %get-tuple-element.69) | copy-start | bytes 24580
  256.5 3.4 %collective-permute-start.8 = (bf16[128,1024]{0,1:T(8,128)(2,1)S(1)}, bf16[128,1024]{0,1:T(8,128)(2,1)S(1)}, u32[]{:S(2)}, u32[]{:S(2)}) collective-permute-start(bf16[128,1024]{0,1:T(8,128)(2,1)S(1)} %broadcast_select_fusion.6), channel_id=1, source_target_pairs={{0,128},{128,0},{1,129},{129,1},{2,130},{130,2},{3,131},{131,3},{4... | collective-permute-start | bytes 786440 | tf_op jit(solution)/shard_map/ppermute | solution.py:17
  (11 other events, 31.5 us)
Sparse Core Ops, SparseCore 0:
  14.5 164.1 all-gather.1
where the time goes:
time: 269 us; the launch traced here: 268 us
  waiting for transfers between devices  151 us (56%)
  starting transfers between devices  37.8 us (14%)
  matrix products  33.7 us (13%)
  other arithmetic  17.5 us (7%)
  between operations  14.8 us (6%)
  local copies, waits for them, and re-layouts  12.9 us (5%)
    all_to_all x2, waiting for transfers between devices, exchange(): lax.all_to_all(filled, 'dp', split_axis=0, concat_axis=0, tiled=True)  81.1 us
    all_gather x1, waiting for transfers between devices, shards(): gathered = lax.all_gather(both, 'dp', axis=0, tiled=True)  69 us
    dot_general x15, matrix products, mm(): return jnp.dot(a, b, preferred_element_type=F32)  32.7 us
    all_to_all x2, starting transfers between devices, exchange(): lax.all_to_all(filled, 'dp', split_axis=0, concat_axis=0, tiled=True)  23.9 us
    ppermute x9, starting transfers between devices, swap(): return lax.ppermute(value, 'pipe', [(0, 1), (1, 0)])  13.8 us
    select_n x13, other arithmetic, pick(): return jnp.where(first_core, a, b)  6.67 us
  transfers between devices with their start and end apart: 12, of which 5 were waited for; matrix products, arithmetic and copies ran while one was open for 19% of the time, Pallas kernels for 0%

commit v1 on v0

--- a/solution.py
+++ b/solution.py
@@ -1,3 +1,4 @@
+import functools
 import jax
 import jax.numpy as jnp
 from jax import lax
@@ -11,6 +12,16 @@
 META = 128
 BF = jnp.bfloat16
 F32 = jnp.float32
+
+
+def save_sums_all(xin, peer_axis):
+    a_next = jnp.stack([xin for _ in range(lax.psum(1, peer_axis))])
+    clean = lax.all_to_all(a_next, axis_name=peer_axis, split_axis=0, concat_axis=0)
+    prior = jnp.concatenate(clean, 0)
+    return prior
+
+
+zones_arrange = functools.partial(save_sums_all, peer_axis="dp")
 
 
 def swap(value):
@@ -94,7 +105,7 @@
     kept = pick(low, high)
     got = swap(pick(high, low))
     both = jnp.concatenate([pick(kept, got), pick(got, kept)], axis=1)
-    gathered = lax.all_gather(both, "dp", axis=0, tiled=True)
+    gathered = zones_arrange(both)
     vectors = jnp.concatenate([ln_gain[0], ln_bias[0], qkv_bias[0], out_bias[0]])
     vectors_got = swap(vectors)
     vectors_of = (pick(vectors, vectors_got), pick(vectors_got, vectors))

time: 269 us -> 551 us (2.05); the launches traced: 268 us -> 543 us
  waiting for transfers between devices: 151 us -> 422 us
  between operations: 14.8 us -> 1.74 us
  starting transfers between devices: 37.8 us -> 49.7 us
  local copies, waits for them, and re-layouts: 12.9 us -> 18.6 us
    all_to_all x0 -> x1, waiting for transfers between devices: none -> 354 us  [save_sums_all(): lax.all_to_all(a_next, axis_name=peer_axis, split_axis=0, concat_axis=0)]
    all_gather x1 -> x0, waiting for transfers between devices: 69 us -> none  [shards(): gathered = lax.all_gather(both, 'dp', axis=0, tiled=True)]
    all_to_all x2, waiting for transfers between devices: 81.1 us -> 66.4 us  [exchange(): lax.all_to_all(filled, 'dp', split_axis=0, concat_axis=0, tiled=True)]
    all_to_all x0 -> x1, starting transfers between devices: none -> 7.73 us  [save_sums_all(): lax.all_to_all(a_next, axis_name=peer_axis, split_axis=0, concat_axis=0)]
    another operation x0 -> x1, local copies, waits for them, and re-layouts: none -> 6.01 us  [save_sums_all(): a_next = jnp.stack([xin for _ in range(lax.psum(1, peer_axis))])]
  transfers between devices with their start and end apart: 12 -> 12, of which waited for: 5 -> 5; matrix products, arithmetic and copies ran while one was open for 19% -> 8% of each run, Pallas kernels for 0% -> 0%
where the time goes in v1:
time: 551 us; the launch traced here: 543 us
  waiting for transfers between devices  422 us (77%)
  starting transfers between devices  49.7 us (9%)
  matrix products  33.6 us (6%)
  local copies, waits for them, and re-layouts  18.6 us (3%)
  other arithmetic  17.5 us (3%)
    all_to_all x1, waiting for transfers between devices, save_sums_all(): lax.all_to_all(a_next, axis_name=peer_axis, split_axis=0, concat_axis=0)  354 us
    all_to_all x2, waiting for transfers between devices, exchange(): lax.all_to_all(filled, 'dp', split_axis=0, concat_axis=0, tiled=True)  66.4 us
    dot_general x15, matrix products, mm(): return jnp.dot(a, b, preferred_element_type=F32)  32.7 us
    all_to_all x2, starting transfers between devices, exchange(): lax.all_to_all(filled, 'dp', split_axis=0, concat_axis=0, tiled=True)  24.5 us
    ppermute x9, starting transfers between devices, swap(): return lax.ppermute(value, 'pipe', [(0, 1), (1, 0)])  17.5 us
  transfers between devices with their start and end apart: 12, of which 5 were waited for; matrix products, arithmetic and copies ran while one was open for 8% of the time, Pallas kernels for 0%

profile of v1, /device:TPU:1, one launch (start us, length us, event | category | flops | bytes accessed | tf_op | source)
XLA Modules:
  0.0 543.1 jit_solution(3244669355442367496)
XLA Ops:
  0.6 1.3 copy.29
  4.0 2.2 fusion.12
  6.2 16.3 %all-to-all-start.1 = ((bf16[128,8,1152]{2,1,0:T(8,128)(2,1)}), bf16[128,8,1152]{2,1,0:T(8,128)(2,1)S(1)}, u32[]{:S(2)}, u32[]{:S(2)}) async-start(bf16[128,8,1152]{2,1,0:T(8,128)(2,1)} %fusion.12), calls=%async_computation.1 | async-start | bytes 4718592 | tf_op jit(solution)/shard_map/all_to_all | solution.py:157
  23.2 1.0 collective-permute-start.1
  24.3 0.9 collective-permute-done.1
  25.2 55.6 %all-to-all-done.1 = bf16[128,8,1152]{2,1,0:T(8,128)(2,1)S(1)} async-done(((bf16[128,8,1152]{2,1,0:T(8,128)(2,1)}), bf16[128,8,1152]{2,1,0:T(8,128)(2,1)S(1)}, u32[]{:S(2)}, u32[]{:S(2)}) %all-to-all-start.1) | async-done | bytes 2359328 | tf_op jit(solution)/shard_map/all_to_all | solution.py:157
  80.8 6.0 %stack.2 = bf16[128,16,4096]{2,1,0:T(8,128)(2,1)} broadcast(bf16[16,4096]{1,0:T(8,128)(2,1)S(1)} %pad_maximum_fusion.20), dimensions={1,2} | broadcast | bytes 16908288 | tf_op jit(solution)/shard_map/stack | solution.py:18
  86.8 7.7 %all-to-all-start = ((bf16[128,16,4096]{2,1,0:T(8,128)(2,1)}), bf16[128,16,4096]{2,1,0:T(8,128)(2,1)}, u32[]{:S(2)}, u32[]{:S(2)}) async-start(bf16[128,16,4096]{2,1,0:T(8,128)(2,1)} %stack.2), calls=%async_computation | async-start | bytes 33554432 | tf_op jit(solution)/shard_map/all_to_all | solution.py:19
  94.6 2.8 collective-permute-start
  99.3 1.0 convolution_convert_fusion.1
  100.3 0.9 collective-permute-start.6
  104.4 354.4 %all-to-all-done = bf16[128,16,4096]{2,1,0:T(8,128)(2,1)} async-done(((bf16[128,16,4096]{2,1,0:T(8,128)(2,1)}), bf16[128,16,4096]{2,1,0:T(8,128)(2,1)}, u32[]{:S(2)}, u32[]{:S(2)}) %all-to-all-start) | async-done | bytes 16777248 | tf_op jit(solution)/shard_map/all_to_all | solution.py:19
  458.8 3.9 fusion.273
  462.7 5.6 %fusion.281 = (bf16[128,1536]{0,1:T(8,128)(2,1)S(1)}, f32[128,1536]{0,1:T(8,128)S(1)}) fusion(f32[1536]{0:T(1024)S(1)} %select_n.239, bf16[2048,4096]{1,0:T(8,128)(2,1)} %bitcast.6, bf16[128,2048]{0,1:T(8,128)(2,1)S(1)} %copy-done.6, f32[2048]{0:T(1024)S(1)} %get-tuple-element.73, f32[2048]{0:T(1024)S(1)} %get-tuple-element.71, f32[128]{0:T(128)S(1)} %rsqrt.36, ...), kind=kOutput, calls=%fused_computation.381 | convolution fusion | flops 807272448 | bytes 8018944 | tf_op jit(solution)/shard_map/dot_general | solution.py:32
  469.5 1.4 fusion.40
  470.9 8.1 %all-to-all-start.2 = ((bf16[128,8,512]{2,1,0:T(8,128)(2,1)}), bf16[128,8,512]{2,1,0:T(8,128)(2,1)}, u32[]{:S(2)}, u32[]{:S(2)}) async-start(bf16[128,8,512]{2,1,0:T(8,128)(2,1)} %fusion.40), calls=%async_computation.2 | async-start | bytes 2097152 | tf_op jit(solution)/shard_map/all_to_all | solution.py:157
  479.2 1.7 pad_maximum_fusion.17
  480.9 4.7 collective-permute-start.3
  486.5 1.6 pad_maximum_fusion.18
  488.6 5.1 fusion.288
  494.4 10.8 %all-to-all-done.2 = bf16[128,8,512]{2,1,0:T(8,128)(2,1)} async-done(((bf16[128,8,512]{2,1,0:T(8,128)(2,1)}), bf16[128,8,512]{2,1,0:T(8,128)(2,1)}, u32[]{:S(2)}, u32[]{:S(2)}) %all-to-all-start.2) | async-done | bytes 1048608 | tf_op jit(solution)/shard_map/all_to_all | solution.py:157
  505.2 1.5 convolution_convert_fusion.3
  506.8 6.5 %collective-permute-start.7 = (bf16[128,512]{1,0:T(8,128)(2,1)S(1)}, bf16[128,512]{1,0:T(8,128)(2,1)S(1)}, u32[]{:S(2)}, u32[]{:S(2)}) collective-permute-start(bf16[128,512]{1,0:T(8,128)(2,1)S(1)} %convolution_convert_fusion.3), channel_id=1, source_target_pairs={{0,128},{128,0},{1,129},{129,1},{2,130},{130,2},{3,131},{131,3},{4... | collective-permute-start | bytes 393224 | tf_op jit(solution)/shard_map/ppermute | solution.py:28
  513.3 3.0 broadcast_select_fusion.3
  516.3 1.8 convert_reduce_fusion.1
  518.4 5.6 %fusion.284 = (bf16[128,1536]{0,1:T(8,128)(2,1)S(1)}, f32[128,1536]{0,1:T(8,128)S(1)}) fusion(f32[1536]{0:T(1024)S(1)} %select_n.250, bf16[2048,4096]{1,0:T(8,128)(2,1)} %bitcast.6, bf16[128,2048]{0,1:T(8,128)(2,1)S(1)} %get-tuple-element.95, f32[2048]{0:T(1024)S(1)} %copy-done.20, f32[2048]{0:T(1024)S(1)} %copy-done.19, f32[128]{0:T(128)S(1)} %add_rsqrt_fusion.3, ...), kind=kOutput, calls=%fused_computation.384 | convolution fusion | flops 807272448 | bytes 8018944 | tf_op jit(solution)/shard_map/dot_general | solution.py:32
  525.6 2.6 broadcast_select_fusion.1
  528.3 1.8 fusion.287
  530.4 4.2 fusion.289
  539.0 1.7 fusion.37
  540.7 1.0 copy.36
  541.9 1.0 copy.43
  (171 shorter events, 17.5 us)
Async XLA Ops:
  2.0 20.6 %copy-start.11 = (bf16[1,16,3072]{2,1,0:T(8,128)(2,1)S(1)}, bf16[1,16,3072]{2,1,0:T(8,128)(2,1)}, u32[]{:S(2)}) copy-start(bf16[1,16,3072]{2,1,0:T(8,128)(2,1)} %param.14) | copy-start | bytes 294916
  2.9 466.1 %copy-start.28 = (s32[128]{0:T(128)}, s32[128]{0:T(128)S(1)}, u32[]{:S(2)}) copy-start(s32[128]{0:T(128)S(1)} %get-tuple-element.110) | copy-start | bytes 1540
  3.7 465.3 %copy-start.26 = (s32[128]{0:T(128)}, s32[128]{0:T(128)S(1)}, u32[]{:S(2)}) copy-start(s32[128]{0:T(128)S(1)} %eq.107) | copy-start | bytes 1540
  3.8 464.5 %copy-start.32 = (f32[128]{0:T(128)}, f32[128]{0:T(128)S(1)}, u32[]{:S(2)}) copy-start(f32[128]{0:T(128)S(1)} %get-tuple-element.12) | copy-start | bytes 1540
  3.8 18.8 %copy-start.34 = (s32[128]{0:T(128)}, s32[128]{0:T(128)S(1)}, u32[]{:S(2)}) copy-start(s32[128]{0:T(128)S(1)} %add_add_fusion) | copy-start | bytes 1540
  3.9 19.3 %copy-start.16 = (bf16[1,8,2048]{2,1,0:T(8,128)(2,1)S(1)}, bf16[1,8,2048]{2,1,0:T(8,128)(2,1)}, u32[]{:S(2)}) copy-start(bf16[1,8,2048]{2,1,0:T(8,128)(2,1)} %param.16) | copy-start | bytes 98308
  6.2 74.6 %all-to-all-start.1 = ((bf16[128,8,1152]{2,1,0:T(8,128)(2,1)}), bf16[128,8,1152]{2,1,0:T(8,128)(2,1)S(1)}, u32[]{:S(2)}, u32[]{:S(2)}) async-start(bf16[128,8,1152]{2,1,0:T(8,128)(2,1)} %fusion.12), calls=%async_computation.1 | async-start | bytes 4718592 | tf_op jit(solution)/shard_map/all_to_all | solution.py:157
  23.2 1.9 collective-permute-start.1
  86.8 7.8 %copy-start.12 = (f32[1,3072]{1,0:T(1,128)S(1)}, f32[1,3072]{1,0:T(1,128)}, u32[]{:S(2)}) copy-start(f32[1,3072]{1,0:T(1,128)} %param.15) | copy-start | bytes 36868
  86.8 7.8 %copy-start.13 = (f32[1,2048]{1,0:T(1,128)S(1)}, f32[1,2048]{1,0:T(1,128)}, u32[]{:S(2)}) copy-start(f32[1,2048]{1,0:T(1,128)} %param.17) | copy-start | bytes 24580
  86.8 7.8 %copy-start.14 = (f32[1,2048]{1,0:T(1,128)S(1)}, f32[1,2048]{1,0:T(1,128)}, u32[]{:S(2)}) copy-start(f32[1,2048]{1,0:T(1,128)} %param.13) | copy-start | bytes 24580
  86.8 7.8 %copy-start.15 = (f32[1,2048]{1,0:T(1,128)S(1)}, f32[1,2048]{1,0:T(1,128)}, u32[]{:S(2)}) copy-start(f32[1,2048]{1,0:T(1,128)} %param.12) | copy-start | bytes 24580
  86.8 10.6 %copy-start.2 = (bf16[4,32,2048]{2,1,0:T(8,128)(2,1)S(1)}, bf16[4,32,2048]{2,1,0:T(8,128)(2,1)}, u32[]{:S(2)}) copy-start(bf16[4,32,2048]{2,1,0:T(8,128)(2,1)} %param.9) | copy-start | bytes 1572868
  86.8 371.9 %all-to-all-start = ((bf16[128,16,4096]{2,1,0:T(8,128)(2,1)}), bf16[128,16,4096]{2,1,0:T(8,128)(2,1)}, u32[]{:S(2)}, u32[]{:S(2)}) async-start(bf16[128,16,4096]{2,1,0:T(8,128)(2,1)} %stack.2), calls=%async_computation | async-start | bytes 33554432 | tf_op jit(solution)/shard_map/all_to_all | solution.py:19
  94.6 3.7 collective-permute-start
  99.0 363.7 %copy-start.21 = (f32[2048]{0:T(1024)}, f32[2048]{0:T(1024)S(1)}, u32[]{:S(2)}) copy-start(f32[2048]{0:T(1024)S(1)} %get-tuple-element.71) | copy-start | bytes 24580
  99.0 363.7 %copy-start.23 = (f32[2048]{0:T(1024)}, f32[2048]{0:T(1024)S(1)}, u32[]{:S(2)}) copy-start(f32[2048]{0:T(1024)S(1)} %get-tuple-element.73) | copy-start | bytes 24580
  100.3 3.3 collective-permute-start.6
  470.9 34.3 %all-to-all-start.2 = ((bf16[128,8,512]{2,1,0:T(8,128)(2,1)}), bf16[128,8,512]{2,1,0:T(8,128)(2,1)}, u32[]{:S(2)}, u32[]{:S(2)}) async-start(bf16[128,8,512]{2,1,0:T(8,128)(2,1)} %fusion.40), calls=%async_computation.2 | async-start | bytes 2097152 | tf_op jit(solution)/shard_map/all_to_all | solution.py:157
  479.0 7.3 %copy-start.1 = (bf16[2048,512]{1,0:T(8,128)(2,1)S(1)}, bf16[2048,512]{1,0:T(8,128)(2,1)}, u32[]{:S(2)}) copy-start(bf16[2048,512]{1,0:T(8,128)(2,1)} %get-tuple-element.16) | copy-start | bytes 6291460
  479.2 7.3 %copy-start = (bf16[1024,512]{1,0:T(8,128)(2,1)}, bf16[1024,512]{1,0:T(8,128)(2,1)S(1)}, u32[]{:S(2)}) copy-start(bf16[1024,512]{1,0:T(8,128)(2,1)S(1)} %get-tuple-element.25) | copy-start | bytes 3145732
  480.9 32.4 %collective-permute-start.3 = (bf16[1024,1024]{1,0:T(8,128)(2,1)}, bf16[1024,1024]{1,0:T(8,128)(2,1)}, u32[]{:S(2)}, u32[]{:S(2)}) collective-permute-start(bf16[1024,1024]{1,0:T(8,128)(2,1)} %pad_maximum_fusion.17), channel_id=1, source_target_pairs={{0,128},{128,0},{1,129},{129,1},{2,130},{130,2},{3,131},{131,3},{4... | collective-permute-start | bytes 6291464 | tf_op jit(solution)/shard_map/ppermute | solution.py:28
  486.2 7.5 %collective-permute-start.2 = (bf16[128,512]{1,0:T(8,128)(2,1)S(1)}, bf16[128,512]{1,0:T(8,128)(2,1)S(1)}, u32[]{:S(2)}, u32[]{:S(2)}) collective-permute-start(bf16[128,512]{1,0:T(8,128)(2,1)S(1)} %pad_maximum_fusion.21), channel_id=1, source_target_pairs={{0,128},{128,0},{1,129},{129,1},{2,130},{130,2},{3,131},{131,3},{4... | collective-permute-start | bytes 393224 | tf_op jit(solution)/shard_map/ppermute | solution.py:28
  488.1 37.4 %collective-permute-start.5 = (bf16[1024,1024]{1,0:T(8,128)(2,1)}, bf16[1024,1024]{1,0:T(8,128)(2,1)}, u32[]{:S(2)}, u32[]{:S(2)}) collective-permute-start(bf16[1024,1024]{1,0:T(8,128)(2,1)} %pad_maximum_fusion.18), channel_id=1, source_target_pairs={{0,128},{128,0},{1,129},{129,1},{2,130},{130,2},{3,131},{131,3},{4... | collective-permute-start | bytes 6291464 | tf_op jit(solution)/shard_map/ppermute | solution.py:28
  506.7 9.5 %copy-start.7 = (bf16[128,2048]{0,1:T(8,128)(2,1)S(1)}, bf16[128,2048]{0,1:T(8,128)(2,1)}, u32[]{:S(2)}) copy-start(bf16[128,2048]{0,1:T(8,128)(2,1)} %copy-done.5) | copy-start | bytes 1572868
  506.7 9.5 %copy-start.9 = (bf16[128,512]{1,0:T(8,128)(2,1)S(1)}, bf16[128,512]{1,0:T(8,128)(2,1)}, u32[]{:S(2)}) copy-start(bf16[128,512]{1,0:T(8,128)(2,1)} %get-tuple-element.62) | copy-start | bytes 393220
  506.8 9.5 %copy-start.10 = (bf16[128,512]{1,0:T(8,128)(2,1)S(1)}, bf16[128,512]{1,0:T(8,128)(2,1)}, u32[]{:S(2)}) copy-start(bf16[128,512]{1,0:T(8,128)(2,1)} %get-tuple-element.63) | copy-start | bytes 393220
  506.8 9.5 %copy-start.18 = (f32[2048]{0:T(1024)S(1)}, f32[2048]{0:T(1024)}, u32[]{:S(2)}) copy-start(f32[2048]{0:T(1024)} %get-tuple-element.72) | copy-start | bytes 24580
  506.8 21.4 %collective-permute-start.7 = (bf16[128,512]{1,0:T(8,128)(2,1)S(1)}, bf16[128,512]{1,0:T(8,128)(2,1)S(1)}, u32[]{:S(2)}, u32[]{:S(2)}) collective-permute-start(bf16[128,512]{1,0:T(8,128)(2,1)S(1)} %convolution_convert_fusion.3), channel_id=1, source_target_pairs={{0,128},{128,0},{1,129},{129,1},{2,130},{130,2},{3,131},{131,3},{4... | collective-permute-start | bytes 393224 | tf_op jit(solution)/shard_map/ppermute | solution.py:28
  525.2 13.6 %collective-permute-start.4 = (bf16[128,512]{1,0:T(8,128)(2,1)S(1)}, bf16[128,512]{1,0:T(8,128)(2,1)S(1)}, u32[]{:S(2)}, u32[]{:S(2)}) collective-permute-start(bf16[128,512]{1,0:T(8,128)(2,1)S(1)} %pad_maximum_fusion.22), channel_id=1, source_target_pairs={{0,128},{128,0},{1,129},{129,1},{2,130},{130,2},{3,131},{131,3},{4... | collective-permute-start | bytes 393224 | tf_op jit(solution)/shard_map/ppermute | solution.py:28
  530.4 8.6 %copy-start.17 = (f32[2048]{0:T(1024)S(1)}, f32[2048]{0:T(1024)}, u32[]{:S(2)}) copy-start(f32[2048]{0:T(1024)} %get-tuple-element.69) | copy-start | bytes 24580
  538.3 3.4 collective-permute-start.8
  (16 other events, 65.8 us)
